TPU v7x, 32 devices: a whole 2x2x4 slice. The times are simulated.
32 devices in a mesh: vocab: 4 (over z), expert: 8 (over y, x, core).
Axes of the slice: x: 2, y: 2, z: 4, core: 2. Of those that a mesh axis runs over, the one named last changes fastest.
Arguments:
- token_ids: int32 [1024], replicated, may hold values from 0 to 75967
- word_mask: int32 [75968], P('vocab'), may hold values 0 or 1
- embed_table: bfloat16 [75968, 4096], P('vocab', 'expert'), may hold values from -6 to 6
- attn_out: bfloat16 [1024, 4096], P('expert', 'vocab'), may hold values from -6 to 6
- in_gain: float32 [4096], replicated, may hold values from 0.25 to 1.75
- key_weight: bfloat16 [4096, 512], P(None, 'vocab'), may hold values from -0.09375 to 0.09375
- key_gain: float32 [128], replicated, may hold values from 0.25 to 1.75
- post_gain: float32 [4096], replicated, may hold values from 0.25 to 1.75
- routes: int32 [1024, 8], P('expert'), may hold values from 0 to 15, all different within a row; in each aligned block of 128 rows (0 to 127, 128 to 255, ...) at most 96 rows name the same one
- gate_ints: int32 [1024, 8], P('expert'), may hold values from 1 to 63
- w_gate: bfloat16 [32, 4096, 768], P(('expert', 'vocab')), may hold values from -0.09375 to 0.09375
- w_up: bfloat16 [32, 4096, 768], P(('expert', 'vocab')), may hold values from -0.09375 to 0.09375
- w_down: bfloat16 [32, 768, 4096], P(('expert', 'vocab')), may hold values from -0.15625 to 0.15625
Outputs:
- expert_out: bfloat16 [1024, 4096], P('expert', 'vocab')
- key_heads: bfloat16 [1024, 512], P('expert', 'vocab')
Inputs may be any that keep to these rules, and one draw needn't show every extreme that they name: `routes`: each row names 8 different experts; within the 128 rows of one index of expert no expert is named by more than 96 rows, and in some such blocks one is named by exactly 96.
All inputs are finite; a program needn't handle non-finite values. No bound on the sum of `word_mask` on one device may be relied on, other than what follows from the above.
Results may differ from a plain program's by a relative error of at most 0.008.
Values may be sent and summed in bfloat16 or wider, within the bound.
A program may use at most 192 MiB of HBM per device.

v0:
```python
import jax
import jax.numpy as jnp
from jax import lax
from jax.sharding import PartitionSpec as P


def rms_rows(values, scale_gain):
    inverse_rms = lax.rsqrt(jnp.mean(values * values, axis=-1, keepdims=True) + 1e-06)
    return values * inverse_rms * scale_gain


def on_device(
    token_ids,
    word_mask,
    embed_table,
    attn_out,
    in_gain,
    key_weight,
    key_gain,
    post_gain,
    routes,
    gate_ints,
    w_gate,
    w_up,
    w_down,
):
    n_vocab = lax.axis_size("vocab")
    n_expert = lax.axis_size("expert")
    vocab_rows = embed_table.shape[0]
    experts_total = n_expert * n_vocab // 2
    whole_mesh = ("expert", "vocab")
    my_vocab = lax.axis_index("vocab")
    my_expert = (lax.axis_index("expert") * n_vocab + my_vocab) // 2
    gate_share = gate_ints.astype(jnp.float32) / jnp.sum(gate_ints, axis=1, keepdims=True).astype(
        jnp.float32
    )
    onehot = routes[:, :, None] == jnp.arange(experts_total, dtype=jnp.int32)[None, None, :]
    share_of = jnp.sum(jnp.where(onehot, gate_share[:, :, None], 0.0), axis=1)
    all_shares = lax.all_gather(share_of, "expert", axis=0, tiled=True)
    my_share = lax.dynamic_slice_in_dim(all_shares, my_expert, 1, axis=1)
    attn_rows = lax.all_to_all(attn_out, "vocab", split_axis=0, concat_axis=1, tiled=True)
    local_ids = token_ids - my_vocab * vocab_rows
    inside = (local_ids >= 0) & (local_ids < vocab_rows)
    safe_ids = jnp.clip(local_ids, 0, vocab_rows - 1)
    keep_row = inside & (word_mask[safe_ids] == 1)
    partial_value = jnp.where(
        keep_row[:, None], embed_table[safe_ids], jnp.zeros_like(embed_table[:1])
    )
    moved_rows = lax.all_to_all(partial_value, "expert", split_axis=0, concat_axis=1, tiled=True)
    rows = lax.psum_scatter(moved_rows, "vocab", scatter_dimension=0, tiled=True)
    rows = rows.astype(jnp.float32)
    mid_rows = (rows + attn_rows.astype(jnp.float32)).astype(jnp.bfloat16)
    expert_in = rms_rows(mid_rows.astype(jnp.float32), post_gain).astype(jnp.bfloat16)
    tokens_in = lax.all_gather(expert_in, whole_mesh, axis=0, tiled=True)
    normed_rows = rms_rows(rows, in_gain).astype(jnp.bfloat16)
    key_rows = lax.all_gather(normed_rows, "vocab", axis=0, tiled=True)
    raw_keys = jnp.dot(key_rows, key_weight, preferred_element_type=jnp.float32)
    key_heads = rms_rows(raw_keys, key_gain).astype(jnp.bfloat16)
    gate_val = jnp.dot(tokens_in, w_gate[0], preferred_element_type=jnp.float32)
    up_val = jnp.dot(tokens_in, w_up[0], preferred_element_type=jnp.float32)
    hidden = (jax.nn.silu(gate_val) * up_val).astype(jnp.bfloat16)
    parts = jnp.dot(hidden, w_down[0], preferred_element_type=jnp.float32)
    weighted = (parts * my_share).astype(jnp.bfloat16)
    by_tokens = lax.psum_scatter(weighted, "expert", scatter_dimension=0, tiled=True)
    expert_out = lax.psum_scatter(by_tokens, "vocab", scatter_dimension=1, tiled=True)
    return (expert_out, key_heads)


def solution(mesh):
    return jax.shard_map(
        on_device,
        mesh=mesh,
        in_specs=(
            P(),
            P("vocab"),
            P("vocab", "expert"),
            P("expert", "vocab"),
            P(),
            P(None, "vocab"),
            P(),
            P(),
            P("expert", None),
            P("expert", None),
            P(("expert", "vocab"), None, None),
            P(("expert", "vocab"), None, None),
            P(("expert", "vocab"), None, None),
        ),
        out_specs=(P("expert", "vocab"), P("expert", "vocab")),
        check_vma=False,
    )
```

profile of v0, /device:TPU:0, one launch (start us, length us, event | category | flops | bytes accessed | tf_op | source)
XLA Modules:
  0.0 324.6 jit_solution(1872449881291243474)
XLA Ops:
  7.2 0.0 reduce-scatter.10.cloned.1.call-start
  7.2 0.8 fusion.14
  8.0 5.9 %gather_fusion = s32[1024]{0:T(1024)S(1)} fusion(s32[18992]{0:T(1024)} %param.14, s32[1024]{0:T(1024)S(1)} %fusion.14), kind=kCustom, calls=%fused_computation | custom fusion | bytes 12288 | tf_op jit(solution)/shard_map/gather | solution.py:45
  13.9 0.7 and_bitcast_fusion
  14.6 13.0 %gather_fusion.1 = bf16[1024,512]{1,0:T(8,128)(2,1)S(1)} fusion(bf16[18992,512]{1,0:T(8,128)(2,1)} %param.15, s32[1024]{0:T(1024)S(1)} %fusion.14), kind=kCustom, calls=%fused_computation.1 | custom fusion | bytes 2101248 | tf_op jit(solution)/shard_map/gather | solution.py:47
  27.7 0.7 copy.30
  28.4 0.1 broadcast_select_fusion
  28.5 20.3 %all_to_all.29 = bf16[8,128,512]{1,2,0:T(8,128)(2,1)S(1)} all-to-all(bf16[8,128,512]{1,2,0:T(8,128)(2,1)S(1)} %broadcast_select_fusion), channel_id=1, replica_groups=mesh['vocab'=4,'expert'=8] {'expert'}, dimensions={0} | all-to-all | bytes 2097152 | tf_op jit(solution)/shard_map/all_to_all | solution.py:49
  48.8 1.3 copy.34
  50.1 0.0 reduce-scatter.10.cloned.1.call-update
  50.1 0.0 all-gather.3.cloned.1.call-start
  50.2 19.2 %all_to_all.30 = bf16[4,32,1024]{2,1,0:T(8,128)(2,1)S(1)} all-to-all(bf16[4,32,1024]{2,1,0:T(8,128)(2,1)S(1)} %bitcast.33), channel_id=1, replica_groups=mesh['vocab'=4,'expert'=8] {'vocab'}, dimensions={0} | all-to-all | bytes 524288 | tf_op jit(solution)/shard_map/all_to_all | solution.py:41
  69.5 10.3 %reduce-scatter.10.cloned.1.call-done = bf16[32,4096]{1,0:T(8,128)(2,1)} async-done(((bf16[128,4096]{1,0:T(8,128)(2,1)}), bf16[32,4096]{1,0:T(8,128)(2,1)}) %reduce-scatter.10.cloned.1.call-update) | async-done | bytes 262160 | tf_op jit(solution)/shard_map/reduce_scatter | solution.py:50
  79.8 1.2 fusion.11
  81.0 1.9 fusion.13
  82.9 0.0 all-gather.3.cloned.1.call-update
  82.9 0.0 reduce-scatter.6.cloned.1.call-start
  83.1 9.1 %all_gather.10 = f32[1024,16]{0,1:T(8,128)S(1)} all-gather(f32[128,16]{0,1:T(8,128)S(1)} %select_reduce_fusion), channel_id=1, replica_groups=mesh['vocab'=4,'expert'=8] {'expert'}, dimensions={0}, use_global_device_ids=true | all-gather | bytes 73728 | tf_op jit(solution)/shard_map/all_gather | solution.py:39
  92.2 67.2 %all-gather.3.cloned.1.call-done = bf16[1024,4096]{1,0:T(8,128)(2,1)} async-done(((bf16[32,4096]{1,0:T(8,128)(2,1)}), bf16[1024,4096]{1,0:T(8,128)(2,1)}) %all-gather.3.cloned.1.call-update) | async-done | bytes 8388624 | tf_op jit(solution)/shard_map/all_gather | solution.py:54
  159.3 11.0 %fusion.1 = f32[1024,768]{1,0:T(8,128)S(1)} fusion(bf16[1024,4096]{1,0:T(8,128)(2,1)} %all-gather.3.cloned.1.call-done, bf16[1,4096,768]{2,1,0:T(8,128)(2,1)} %param.24), kind=kOutput, calls=%fused_computation.4 | convolution fusion | flops 6442450944 | bytes 17825792 | tf_op jit(solution)/shard_map/dot_general | solution.py:60
  170.4 9.9 %multiply_convert_fusion.1 = bf16[1024,768]{1,0:T(8,128)(2,1)S(1)} fusion(f32[1024,768]{1,0:T(8,128)S(1)} %fusion.1, bf16[1024,4096]{1,0:T(8,128)(2,1)S(1)} %copy-done.7, bf16[1,4096,768]{2,1,0:T(8,128)(2,1)} %param.23), kind=kOutput, calls=%fused_computation.8 | convolution fusion | flops 6447169536 | bytes 19398656 | tf_op jit(solution)/shard_map/dot_general | solution.py:59
  180.4 8.9 %multiply_convert_fusion = bf16[1024,4096]{1,0:T(8,128)(2,1)} fusion(f32[1024]{0:T(1024)S(1)} %bitcast.34, bf16[1024,768]{1,0:T(8,128)(2,1)S(1)} %multiply_convert_fusion.1, bf16[1,768,4096]{2,1,0:T(8,128)(2,1)S(1)} %bitcast.36), kind=kOutput, calls=%fused_computation.2 | convolution fusion | flops 6450839552 | bytes 16257024 | tf_op jit(solution)/shard_map/dot_general | solution.py:62
  189.2 0.0 reduce-scatter.6.cloned.1.call-update
  189.3 0.0 all-gather.5.cloned.1.call-start
  189.3 0.5 all-gather.5.cloned.1.call-update
  189.8 0.0 reduce-scatter.8.cloned.1.call-start
  189.9 69.4 %reduce-scatter.6.cloned.1.call-done = bf16[128,4096]{1,0:T(8,128)(2,1)} async-done(((bf16[1024,4096]{1,0:T(8,128)(2,1)}), bf16[128,4096]{1,0:T(8,128)(2,1)}) %reduce-scatter.6.cloned.1.call-update) | async-done | bytes 1048592 | tf_op jit(solution)/shard_map/reduce_scatter | solution.py:64
  259.3 29.4 %all-gather.5.cloned.1.call-done = bf16[128,4096]{1,0:T(8,128)(2,1)} async-done(((bf16[32,4096]{1,0:T(8,128)(2,1)}), bf16[128,4096]{1,0:T(8,128)(2,1)}) %all-gather.5.cloned.1.call-update) | async-done | bytes 1048592 | tf_op jit(solution)/shard_map/all_gather | solution.py:56
  288.7 1.8 multiply_reduce_fusion
  290.5 0.1 multiply_convert_fusion.2
  290.6 0.7 copy.33
  291.3 26.8 %reduce-scatter.8.cloned.1.call-done = bf16[128,1024]{1,0:T(8,128)(2,1)} async-done(((bf16[128,4096]{1,0:T(8,128)(2,1)}), bf16[128,1024]{1,0:T(8,128)(2,1)}) %reduce-scatter.8.cloned.1.call-update) | async-done | bytes 262160 | tf_op jit(solution)/shard_map/reduce_scatter | solution.py:65
  (31 shorter events, 0.2 us)
Async XLA Ops:
  7.2 281.5 %copy-start = (bf16[4096,128]{1,0:T(8,128)(2,1)S(1)}, bf16[4096,128]{1,0:T(8,128)(2,1)}, u32[]{:S(2)}) copy-start(bf16[4096,128]{1,0:T(8,128)(2,1)} %param.18) | copy-start | bytes 3145732
  7.2 72.6 %reduce-scatter.10.cloned.1.call-start = ((), (), s32[]{:S(2)}) async-start(), calls=%async_computation.9 | async-start | bytes 1310720 | tf_op jit(solution)/shard_map/reduce_scatter | solution.py:50
  27.7 22.5 %copy-start.1 = (bf16[128,1024]{1,0:T(8,128)(2,1)S(1)}, bf16[128,1024]{1,0:T(8,128)(2,1)}, u32[]{:S(2)}) copy-start(bf16[128,1024]{1,0:T(8,128)(2,1)} %param.16) | copy-start | bytes 786436
  27.7 53.3 %copy-start.2 = (f32[4096]{0:T(1024)S(1)}, f32[4096]{0:T(1024)}, u32[]{:S(2)}) copy-start(f32[4096]{0:T(1024)} %param.17) | copy-start | bytes 49156
  27.7 53.3 %copy-start.3 = (f32[4096]{0:T(1024)S(1)}, f32[4096]{0:T(1024)}, u32[]{:S(2)}) copy-start(f32[4096]{0:T(1024)} %param.20) | copy-start | bytes 49156
  28.4 54.6 %copy-start.4 = (s32[128,8]{0,1:T(8,128)S(1)}, s32[128,8]{0,1:T(8,128)}, u32[]{:S(2)}) copy-start(s32[128,8]{0,1:T(8,128)} %param.22) | copy-start | bytes 12292
  28.4 54.7 %copy-start.5 = (s32[128,8]{0,1:T(8,128)S(1)}, s32[128,8]{0,1:T(8,128)}, u32[]{:S(2)}) copy-start(s32[128,8]{0,1:T(8,128)} %param.21) | copy-start | bytes 12292
  50.1 109.2 %all-gather.3.cloned.1.call-start = ((), (), s32[]{:S(2)}) async-start(), calls=%async_computation.5 | async-start | bytes 8650752 | tf_op jit(solution)/shard_map/all_gather | solution.py:54
  82.9 176.4 %reduce-scatter.6.cloned.1.call-start = ((), (), s32[]{:S(2)}) async-start(), calls=%async_computation.6 | async-start | bytes 9437184 | tf_op jit(solution)/shard_map/reduce_scatter | solution.py:64
  159.3 11.1 %copy-start.7 = (bf16[1024,4096]{1,0:T(8,128)(2,1)S(1)}, bf16[1024,4096]{1,0:T(8,128)(2,1)}, u32[]{:S(2)}) copy-start(bf16[1024,4096]{1,0:T(8,128)(2,1)} %all-gather.3.cloned.1.call-done) | copy-start | bytes 25165828
  159.3 21.0 %slice-start = ((s8[6291456]{0:T(1024)(128)(4,1)}), s8[4194304]{0:T(1024)(128)(4,1)S(1)}, s32[]{:S(2)}) async-start(s8[6291456]{0:T(1024)(128)(4,1)} %bitcast.35), calls=%async_computation.10 | async-start | bytes 8388608
  170.4 10.0 %slice-start.1 = ((s8[6291456]{0:T(1024)(128)(4,1)}), s8[2097152]{0:T(1024)(128)(4,1)S(1)}, s32[]{:S(2)}) async-start(s8[6291456]{0:T(1024)(128)(4,1)} %bitcast.35), calls=%async_computation.11 | async-start | bytes 4194304
  189.2 101.2 %copy-start.6 = (f32[128]{0:T(128)S(1)}, f32[128]{0:T(128)}, u32[]{:S(2)}) copy-start(f32[128]{0:T(128)} %param.19) | copy-start | bytes 1540
  189.3 99.4 %all-gather.5.cloned.1.call-start = ((), (), s32[]{:S(2)}) async-start(), calls=%async_computation.8 | async-start | bytes 1310720 | tf_op jit(solution)/shard_map/all_gather | solution.py:56
  189.8 128.2 %reduce-scatter.8.cloned.1.call-start = ((), (), s32[]{:S(2)}) async-start(), calls=%async_computation.7 | async-start | bytes 1310720 | tf_op jit(solution)/shard_map/reduce_scatter | solution.py:65
Sparse Core Ops, SparseCore 0:
  50.2 29.4 reduce-scatter.9
  83.7 75.5 all-gather.2
  189.4 69.8 reduce-scatter.5
  260.7 27.9 all-gather.4
  291.4 26.6 reduce-scatter.7
where the time goes:
time: 325 us
  waiting for transfers between devices  204 us (63%)
  blocking collectives  48.6 us (15%)
  matrix products  31.6 us (10%)
  local copies, waits for them, and re-layouts  21.7 us (7%)
  between operations  14 us (4%)
  other arithmetic  4.83 us (1%)
    reduce_scatter x1, waiting for transfers between devices, on_device(): lax.psum_scatter(weighted, 'expert', scatter_dimension=0, tiled=True)  69.4 us
    all_gather x1, waiting for transfers between devices, on_device(): tokens_in = lax.all_gather(expert_in, whole_mesh, axis=0, tiled=True)  67.2 us
    all_gather x1, waiting for transfers between devices, on_device(): key_rows = lax.all_gather(normed_rows, 'vocab', axis=0, tiled=True)  29.4 us
    reduce_scatter x1, waiting for transfers between devices, on_device(): lax.psum_scatter(by_tokens, 'vocab', scatter_dimension=1, tiled=True)  26.8 us
    all_to_all x1, blocking collectives, on_device(): lax.all_to_all(partial_value, 'expert', split_axis=0, concat_axis=1, tile...  20.3 us
    all_to_all x1, blocking collectives, on_device(): lax.all_to_all(attn_out, 'vocab', split_axis=0, concat_axis=1, tiled=True)  19.2 us
    gather x2, local copies, waits for them, and re-layouts, on_device(): embed_table[safe_ids]  13.7 us
    dot_general x1, matrix products, on_device(): up_val = jnp.dot(tokens_in, w_up[0], preferred_element_type=jnp.float32)  11 us
  transfers between devices with their start and end apart: 5, of which 5 were waited for; matrix products, arithmetic and copies ran while one was open for 1% of the time, Pallas kernels for 0%

commit v1 on v0

--- a/solution.py
+++ b/solution.py
@@ -53,7 +53,25 @@
     expert_in = rms_rows(mid_rows.astype(jnp.float32), post_gain).astype(jnp.bfloat16)
     tokens_in = lax.all_gather(expert_in, whole_mesh, axis=0, tiled=True)
     normed_rows = rms_rows(rows, in_gain).astype(jnp.bfloat16)
-    key_rows = lax.all_gather(normed_rows, "vocab", axis=0, tiled=True)
+    size, place, span = (lax.axis_size("vocab"), lax.axis_index("vocab"), normed_rows.shape[0])
+    right = [(i, (i + 1) % size) for i in range(size)]
+    backward = [(i, (i - 1) % size) for i in range(size)]
+    key_rows = jnp.zeros(
+        (*normed_rows.shape[:0], size * span, *normed_rows.shape[0 + 1 :]), normed_rows.dtype
+    )
+    key_rows = lax.dynamic_update_slice_in_dim(key_rows, normed_rows, place * span, axis=0)
+    from_left = from_right = normed_rows
+    middle = size // 2
+    for step in range(1, middle + 1):
+        from_left = lax.ppermute(from_left, "vocab", right)
+        key_rows = lax.dynamic_update_slice_in_dim(
+            key_rows, from_left, (place - step) % size * span, axis=0
+        )
+        if step < size - middle:
+            from_right = lax.ppermute(from_right, "vocab", backward)
+            key_rows = lax.dynamic_update_slice_in_dim(
+                key_rows, from_right, (place + step) % size * span, axis=0
+            )
     raw_keys = jnp.dot(key_rows, key_weight, preferred_element_type=jnp.float32)
     key_heads = rms_rows(raw_keys, key_gain).astype(jnp.bfloat16)
     gate_val = jnp.dot(tokens_in, w_gate[0], preferred_element_type=jnp.float32)

time: 325 us -> 300 us (0.923)
  waiting for transfers between devices: 204 us -> 174 us
  starting transfers between devices: 0.2 us -> 5.09 us
    all_gather x1 -> x0, waiting for transfers between devices: 29.4 us -> none  [on_device(): key_rows = lax.all_gather(normed_rows, 'vocab', axis=0, tiled=True)]
    ppermute x0 -> x3, waiting for transfers between devices: none -> 18.3 us  [the longest x2 10.1 us: on_device(): from_left = lax.ppermute(from_left, 'vocab', right)]
    reduce_scatter x1, waiting for transfers between devices: 26.8 us -> 10.1 us  [on_device(): lax.psum_scatter(by_tokens, 'vocab', scatter_dimension=1, tiled=True)]
    ppermute x0 -> x3, starting transfers between devices: none -> 4.93 us  [the longest x1 3.37 us: on_device(): from_right = lax.ppermute(from_right, 'vocab', backward)]
  transfers between devices with their start and end apart: 5 -> 7, of which waited for: 5 -> 6; matrix products, arithmetic and copies ran while one was open for 1% -> 1% of each run, Pallas kernels for 0% -> 0%
where the time goes in v1:
time: 300 us; the launch traced here: 299 us
  waiting for transfers between devices  174 us (58%)
  blocking collectives  48.6 us (16%)
  matrix products  30.4 us (10%)
  local copies, waits for them, and re-layouts  22.6 us (8%)
  between operations  14.1 us (5%)
  starting transfers between devices  5.09 us (2%)
  other arithmetic  4.81 us (2%)
    reduce_scatter x1, waiting for transfers between devices, on_device(): lax.psum_scatter(weighted, 'expert', scatter_dimension=0, tiled=True)  67.4 us
    all_gather x1, waiting for transfers between devices, on_device(): tokens_in = lax.all_gather(expert_in, whole_mesh, axis=0, tiled=True)  67.3 us
    all_to_all x1, blocking collectives, on_device(): lax.all_to_all(partial_value, 'expert', split_axis=0, concat_axis=1, tile...  20.3 us
    all_to_all x1, blocking collectives, on_device(): lax.all_to_all(attn_out, 'vocab', split_axis=0, concat_axis=1, tiled=True)  19.2 us
    gather x2, local copies, waits for them, and re-layouts, on_device(): embed_table[safe_ids]  13.7 us
    dot_general x1, matrix products, on_device(): up_val = jnp.dot(tokens_in, w_up[0], preferred_element_type=jnp.float32)  11 us
    reduce_scatter x1, waiting for transfers between devices, on_device(): lax.psum_scatter(moved_rows, 'vocab', scatter_dimension=0, tiled=True)  10.3 us
    reduce_scatter x1, waiting for transfers between devices, on_device(): lax.psum_scatter(by_tokens, 'vocab', scatter_dimension=1, tiled=True)  10.1 us
  transfers between devices with their start and end apart: 7, of which 6 were waited for; matrix products, arithmetic and copies ran while one was open for 1% of the time, Pallas kernels for 0%

profile of v1, /device:TPU:0, one launch (start us, length us, event | category | flops | bytes accessed | tf_op | source)
XLA Modules:
  0.0 299.2 jit_solution(8097365811429780878)
XLA Ops:
  7.2 0.8 fusion.14
  8.0 5.9 %gather_fusion = s32[1024]{0:T(1024)S(1)} fusion(s32[18992]{0:T(1024)} %param.14, s32[1024]{0:T(1024)S(1)} %fusion.14), kind=kCustom, calls=%fused_computation | custom fusion | bytes 12288 | tf_op jit(solution)/shard_map/gather | solution.py:45
  13.9 0.7 and_bitcast_fusion
  14.6 13.0 %gather_fusion.1 = bf16[1024,512]{1,0:T(8,128)(2,1)S(1)} fusion(bf16[18992,512]{1,0:T(8,128)(2,1)} %param.15, s32[1024]{0:T(1024)S(1)} %fusion.14), kind=kCustom, calls=%fused_computation.1 | custom fusion | bytes 2101248 | tf_op jit(solution)/shard_map/gather | solution.py:47
  27.7 0.7 copy.30
  28.4 0.1 broadcast_select_fusion
  28.5 20.3 %all_to_all.29 = bf16[8,128,512]{1,2,0:T(8,128)(2,1)S(1)} all-to-all(bf16[8,128,512]{1,2,0:T(8,128)(2,1)S(1)} %broadcast_select_fusion), channel_id=1, replica_groups=mesh['vocab'=4,'expert'=8] {'expert'}, dimensions={0} | all-to-all | bytes 2097152 | tf_op jit(solution)/shard_map/all_to_all | solution.py:49
  48.8 1.3 copy.34
  50.1 0.0 all-gather.2.cloned.1.call-start
  50.2 19.2 %all_to_all.30 = bf16[4,32,1024]{2,1,0:T(8,128)(2,1)S(1)} all-to-all(bf16[4,32,1024]{2,1,0:T(8,128)(2,1)S(1)} %bitcast.33), channel_id=1, replica_groups=mesh['vocab'=4,'expert'=8] {'vocab'}, dimensions={0} | all-to-all | bytes 524288 | tf_op jit(solution)/shard_map/all_to_all | solution.py:41
  69.5 10.3 %reduce-scatter.10.cloned.1.call-done = bf16[32,4096]{1,0:T(8,128)(2,1)} async-done(((bf16[128,4096]{1,0:T(8,128)(2,1)}), bf16[32,4096]{1,0:T(8,128)(2,1)}) %reduce-scatter.10.cloned.1.call-update) | async-done | bytes 262160 | tf_op jit(solution)/shard_map/reduce_scatter | solution.py:50
  79.8 1.2 fusion.11
  81.0 1.8 fusion.9
  82.8 0.0 reduce-scatter.6.cloned.1.call-start
  82.9 9.1 %all_gather.7 = f32[1024,16]{0,1:T(8,128)S(1)} all-gather(f32[128,16]{0,1:T(8,128)S(1)} %select_reduce_fusion), channel_id=1, replica_groups=mesh['vocab'=4,'expert'=8] {'expert'}, dimensions={0}, use_global_device_ids=true | all-gather | bytes 73728 | tf_op jit(solution)/shard_map/all_gather | solution.py:39
  92.0 67.3 %all-gather.2.cloned.1.call-done = bf16[1024,4096]{1,0:T(8,128)(2,1)} async-done(((bf16[32,4096]{1,0:T(8,128)(2,1)}), bf16[1024,4096]{1,0:T(8,128)(2,1)}) %all-gather.2.cloned.1.call-update) | async-done | bytes 8388624 | tf_op jit(solution)/shard_map/all_gather | solution.py:54
  159.3 11.0 %fusion.1 = f32[1024,768]{1,0:T(8,128)S(1)} fusion(bf16[1024,4096]{1,0:T(8,128)(2,1)} %all-gather.2.cloned.1.call-done, bf16[1,4096,768]{2,1,0:T(8,128)(2,1)} %param.24), kind=kOutput, calls=%fused_computation.4 | convolution fusion | flops 6442450944 | bytes 17825792 | tf_op jit(solution)/shard_map/dot_general | solution.py:78
  170.4 9.9 %multiply_convert_fusion.1 = bf16[1024,768]{1,0:T(8,128)(2,1)S(1)} fusion(f32[1024,768]{1,0:T(8,128)S(1)} %fusion.1, bf16[1024,4096]{1,0:T(8,128)(2,1)S(1)} %copy-done.8, bf16[1,4096,768]{2,1,0:T(8,128)(2,1)} %param.23), kind=kOutput, calls=%fused_computation.8 | convolution fusion | flops 6447169536 | bytes 19398656 | tf_op jit(solution)/shard_map/dot_general | solution.py:77
  180.4 8.9 %multiply_convert_fusion = bf16[1024,4096]{1,0:T(8,128)(2,1)} fusion(f32[1024]{0:T(1024)S(1)} %bitcast.34, bf16[1024,768]{1,0:T(8,128)(2,1)S(1)} %multiply_convert_fusion.1, bf16[1,768,4096]{2,1,0:T(8,128)(2,1)S(1)} %bitcast.36), kind=kOutput, calls=%fused_computation.2 | convolution fusion | flops 6450839552 | bytes 16257024 | tf_op jit(solution)/shard_map/dot_general | solution.py:80
  189.3 0.0 reduce-scatter.8.cloned.1.call-start
  189.3 0.1 broadcast_in_dim.55
  189.4 0.8 copy-done.1
  190.2 0.1 constant_dynamic-update-slice_fusion.3
  190.3 1.6 collective-permute-start
  191.9 67.4 %reduce-scatter.6.cloned.1.call-done = bf16[128,4096]{1,0:T(8,128)(2,1)} async-done(((bf16[1024,4096]{1,0:T(8,128)(2,1)}), bf16[128,4096]{1,0:T(8,128)(2,1)}) %reduce-scatter.6.cloned.1.call-update) | async-done | bytes 1048592 | tf_op jit(solution)/shard_map/reduce_scatter | solution.py:82
  259.4 3.4 %collective-permute-start.1 = (bf16[32,4096]{1,0:T(8,128)(2,1)S(1)}, bf16[32,4096]{1,0:T(8,128)(2,1)S(1)}, u32[]{:S(2)}, u32[]{:S(2)}) collective-permute-start(bf16[32,4096]{1,0:T(8,128)(2,1)S(1)} %get-tuple-element.13), channel_id=1, source_target_pairs={{0,24},{8,0},{16,8},{24,16},{1,25},{9,1},{17,9},{25,17},{2,26},{10... | collective-permute-start | bytes 786440 | tf_op jit(solution)/shard_map/ppermute | solution.py:71
  262.8 8.2 %collective-permute-done.1 = bf16[32,4096]{1,0:T(8,128)(2,1)S(1)} collective-permute-done((bf16[32,4096]{1,0:T(8,128)(2,1)S(1)}, bf16[32,4096]{1,0:T(8,128)(2,1)S(1)}, u32[]{:S(2)}, u32[]{:S(2)}) %collective-permute-start.1) | collective-permute-done | bytes 262176 | tf_op jit(solution)/shard_map/ppermute | solution.py:71
  271.0 10.1 %collective-permute-done.2 = bf16[32,4096]{1,0:T(8,128)(2,1)S(1)} collective-permute-done((bf16[32,4096]{1,0:T(8,128)(2,1)S(1)}, bf16[32,4096]{1,0:T(8,128)(2,1)S(1)}, u32[]{:S(2)}, u32[]{:S(2)}) %collective-permute-start.2) | collective-permute-done | bytes 262176 | tf_op jit(solution)/shard_map/ppermute | solution.py:66
  281.1 0.6 multiply_reduce_fusion
  281.7 0.1 multiply_convert_fusion.2
  281.8 0.7 copy.33
  282.5 10.1 %reduce-scatter.8.cloned.1.call-done = bf16[128,1024]{1,0:T(8,128)(2,1)} async-done(((bf16[128,4096]{1,0:T(8,128)(2,1)}), bf16[128,1024]{1,0:T(8,128)(2,1)}) %reduce-scatter.8.cloned.1.call-update) | async-done | bytes 262160 | tf_op jit(solution)/shard_map/reduce_scatter | solution.py:83
  (42 shorter events, 0.4 us)
Async XLA Ops:
  7.2 274.0 %copy-start = (bf16[4096,128]{1,0:T(8,128)(2,1)S(1)}, bf16[4096,128]{1,0:T(8,128)(2,1)}, u32[]{:S(2)}) copy-start(bf16[4096,128]{1,0:T(8,128)(2,1)} %param.18) | copy-start | bytes 3145732
  7.2 72.6 %reduce-scatter.10.cloned.1.call-start = ((), (), s32[]{:S(2)}) async-start(), calls=%async_computation.8 | async-start | bytes 1310720 | tf_op jit(solution)/shard_map/reduce_scatter | solution.py:50
  27.7 22.5 %copy-start.2 = (bf16[128,1024]{1,0:T(8,128)(2,1)S(1)}, bf16[128,1024]{1,0:T(8,128)(2,1)}, u32[]{:S(2)}) copy-start(bf16[128,1024]{1,0:T(8,128)(2,1)} %param.16) | copy-start | bytes 786436
  27.7 53.3 %copy-start.3 = (f32[4096]{0:T(1024)S(1)}, f32[4096]{0:T(1024)}, u32[]{:S(2)}) copy-start(f32[4096]{0:T(1024)} %param.20) | copy-start | bytes 49156
  28.3 54.5 %copy-start.5 = (s32[128,8]{0,1:T(8,128)S(1)}, s32[128,8]{0,1:T(8,128)}, u32[]{:S(2)}) copy-start(s32[128,8]{0,1:T(8,128)} %param.22) | copy-start | bytes 12292
  28.4 54.5 %copy-start.6 = (s32[128,8]{0,1:T(8,128)S(1)}, s32[128,8]{0,1:T(8,128)}, u32[]{:S(2)}) copy-start(s32[128,8]{0,1:T(8,128)} %param.21) | copy-start | bytes 12292
  50.1 109.2 %all-gather.2.cloned.1.call-start = ((), (), s32[]{:S(2)}) async-start(), calls=%async_computation.5 | async-start | bytes 8650752 | tf_op jit(solution)/shard_map/all_gather | solution.py:54
  82.8 176.5 %reduce-scatter.6.cloned.1.call-start = ((), (), s32[]{:S(2)}) async-start(), calls=%async_computation.6 | async-start | bytes 9437184 | tf_op jit(solution)/shard_map/reduce_scatter | solution.py:82
  159.3 11.1 %copy-start.8 = (bf16[1024,4096]{1,0:T(8,128)(2,1)S(1)}, bf16[1024,4096]{1,0:T(8,128)(2,1)}, u32[]{:S(2)}) copy-start(bf16[1024,4096]{1,0:T(8,128)(2,1)} %all-gather.2.cloned.1.call-done) | copy-start | bytes 25165828
  159.3 21.0 %slice-start = ((s8[6291456]{0:T(1024)(128)(4,1)}), s8[4194304]{0:T(1024)(128)(4,1)S(1)}, s32[]{:S(2)}) async-start(s8[6291456]{0:T(1024)(128)(4,1)} %bitcast.35), calls=%async_computation.9 | async-start | bytes 8388608
  170.4 10.0 %slice-start.1 = ((s8[6291456]{0:T(1024)(128)(4,1)}), s8[2097152]{0:T(1024)(128)(4,1)S(1)}, s32[]{:S(2)}) async-start(s8[6291456]{0:T(1024)(128)(4,1)} %bitcast.35), calls=%async_computation.10 | async-start | bytes 4194304
  189.2 0.9 copy-start.1
  189.2 1.0 copy-start.4
  189.2 92.5 %copy-start.7 = (f32[128]{0:T(128)S(1)}, f32[128]{0:T(128)}, u32[]{:S(2)}) copy-start(f32[128]{0:T(128)} %param.19) | copy-start | bytes 1540
  189.3 103.4 %reduce-scatter.8.cloned.1.call-start = ((), (), s32[]{:S(2)}) async-start(), calls=%async_computation.7 | async-start | bytes 1310720 | tf_op jit(solution)/shard_map/reduce_scatter | solution.py:83
  190.3 72.4 %collective-permute-start = (bf16[32,4096]{1,0:T(8,128)(2,1)S(1)}, bf16[32,4096]{1,0:T(8,128)(2,1)S(1)}, u32[]{:S(2)}, u32[]{:S(2)}) collective-permute-start(bf16[32,4096]{1,0:T(8,128)(2,1)S(1)} %get-tuple-element.13), channel_id=1, source_target_pairs={{0,8},{8,16},{16,24},{24,0},{1,9},{9,17},{17,25},{25,1},{2,10},{10... | collective-permute-start | bytes 786440 | tf_op jit(solution)/shard_map/ppermute | solution.py:66
  259.4 11.6 %collective-permute-start.1 = (bf16[32,4096]{1,0:T(8,128)(2,1)S(1)}, bf16[32,4096]{1,0:T(8,128)(2,1)S(1)}, u32[]{:S(2)}, u32[]{:S(2)}) collective-permute-start(bf16[32,4096]{1,0:T(8,128)(2,1)S(1)} %get-tuple-element.13), channel_id=1, source_target_pairs={{0,24},{8,0},{16,8},{24,16},{1,25},{9,1},{17,9},{25,17},{2,26},{10... | collective-permute-start | bytes 786440 | tf_op jit(solution)/shard_map/ppermute | solution.py:71
  262.8 18.4 %collective-permute-start.2 = (bf16[32,4096]{1,0:T(8,128)(2,1)S(1)}, bf16[32,4096]{1,0:T(8,128)(2,1)S(1)}, u32[]{:S(2)}, u32[]{:S(2)}) collective-permute-start(bf16[32,4096]{1,0:T(8,128)(2,1)S(1)} %collective-permute-done), channel_id=1, source_target_pairs={{0,8},{8,16},{16,24},{24,0},{1,9},{9,17},{17,25},{25,1},{2,10},{10... | collective-permute-start | bytes 786440 | tf_op jit(solution)/shard_map/ppermute | solution.py:66
Sparse Core Ops, SparseCore 0:
  50.2 29.4 reduce-scatter.9
  83.7 75.5 all-gather.1
  189.4 69.8 reduce-scatter.5
  262.0 30.6 reduce-scatter.7
